TPU v7x, 32 devices: a whole 2x2x4 slice. The times are simulated.
32 devices in a mesh: req: 8 (over z, y), tp: 4 (over x, core).
Axes of the slice: x: 2, y: 2, z: 4, core: 2. Of those that a mesh axis runs over, the one named last changes fastest.
Arguments:
- tokens: bfloat16 [4096, 2048], P('req')
- token_request_number: int32 [8, 512], P('req'), may hold values from 0 to 7, never falling along the last dimension, each value on 1 to 256 neighbouring positions
- request_adapter_position: int32 [8, 8], P('req'), may hold values from 0 to 15
- adapters_in_use: int32 [16], replicated, may hold values from 0 to 15, as said below
- adapter_storage_slot: int32 [16], replicated, may hold values from 0 to 15, each once
- input_norm_gain: bfloat16 [2048], replicated, may hold values from 0.5 to 1.5
- query_weight: bfloat16 [2048, 2048], P('req', 'tp')
- key_weight: bfloat16 [2048, 2048], P('req', 'tp')
- value_weight: bfloat16 [2048, 2048], P('req', 'tp'), may hold values from -0.125 to 0.125
- output_weight: bfloat16 [2048, 2048], P('tp', 'req'), may hold values from -0.125 to 0.125
- adapter_down_weight: bfloat16 [16, 2, 16, 2048], P('req'), may hold values from -0.125 to 0.125
- adapter_up_weight: bfloat16 [16, 2, 16, 2048], P('req', None, None, 'tp'), may hold values from -0.75 to 0.75
Outputs:
- layer_out: bfloat16 [4096, 2048], P('req', 'tp')
Inputs may be any that keep to these rules, and one draw needn't show every extreme that they name: `adapters_in_use`: 16 different adapter numbers; 0 and 15 are always among them. `token_request_number`: the 512 tokens of each index of req form exactly 8 requests in order, each of 1 to 256 tokens, and one of exactly 256.
All inputs are finite; a program needn't handle non-finite values.
Results may differ from a plain program's by a relative error of at most 0.01.
Values may be sent and summed in bfloat16 or wider, within the bound.
A program may use at most 64 MiB of HBM per device.

v0:
```python
import jax
import jax.numpy as jnp
from jax import lax
from jax.sharding import PartitionSpec as P

HEAD_WIDTH = 64
norm_eps = 1e-05
rope_base = 130000.0
adapter_scale = 2.0


def spread_2(value, axis, root):
    mine = lax.axis_index(axis) == root
    return lax.psum(jnp.where(mine, value, jnp.zeros_like(value)), axis)


def positions_of(segment):
    ordinal = jnp.arange(segment.shape[0], dtype=jnp.int32)
    starts = jnp.concatenate([jnp.ones((1,), jnp.bool_), segment[1:] != segment[:-1]])
    segment_start = lax.cummax(jnp.where(starts, ordinal, jnp.zeros_like(ordinal)), axis=0)
    return ordinal - segment_start


def apply_rotation(values, token_positions):
    half_dim = HEAD_WIDTH // 2
    frequency = rope_base ** (-(jnp.arange(half_dim, dtype=jnp.float32) * 2.0 / HEAD_WIDTH))
    angles = token_positions.astype(jnp.float32)[:, None] * frequency[None, :]
    cosine = jnp.cos(angles)[:, None, :]
    sine_part = jnp.sin(angles)[:, None, :]
    first_half = values[..., :half_dim]
    second_half = values[..., half_dim:]
    return jnp.concatenate(
        [
            first_half * cosine - second_half * sine_part,
            second_half * cosine + first_half * sine_part,
        ],
        axis=-1,
    )


def attend(query_per_head, key_heads, value_per_head, segment):
    scores = (
        jnp.einsum("qhd,khd->hqk", query_per_head, key_heads, preferred_element_type=jnp.float32)
        * 0.125
    )
    ordinal = jnp.arange(segment.shape[0], dtype=jnp.int32)
    allowed = (segment[:, None] == segment[None, :]) & (ordinal[None, :] <= ordinal[:, None])
    scores = jnp.where(allowed[None], scores, jnp.float32(-1e30))
    row_peak = jnp.max(scores, axis=-1, keepdims=True)
    exponent = jnp.where(allowed[None], jnp.exp(scores - row_peak), jnp.float32(0.0))
    weights = (exponent / jnp.sum(exponent, axis=-1, keepdims=True)).astype(jnp.bfloat16)
    return jnp.einsum(
        "hqk,khd->qhd", weights, value_per_head, preferred_element_type=jnp.float32
    ).astype(jnp.bfloat16)


def local(
    tokens,
    token_request_number,
    request_adapter_position,
    adapters_in_use,
    adapter_storage_slot,
    input_norm_gain,
    query_weight,
    key_weight,
    value_weight,
    output_weight,
    adapter_down_weight,
    adapter_up_weight,
):
    row_total, model_width = tokens.shape
    local_width = query_weight.shape[1]
    reduced_rows = adapter_down_weight.shape[2]
    active_count = adapters_in_use.shape[0]
    slot_total = adapter_down_weight.shape[0]
    segment = token_request_number[0]
    request_adapters = request_adapter_position[0]
    storage_slots = jnp.take(adapter_storage_slot, adapters_in_use, axis=0)
    stored_weight = jnp.concatenate([adapter_down_weight, adapter_up_weight], axis=3)

    def fetch_one(active_index, fetched):
        home = storage_slots[active_index]
        own_slot = lax.dynamic_index_in_dim(stored_weight, home % slot_total, 0, keepdims=False)
        received = spread_2(own_slot, "req", home // slot_total)
        return lax.dynamic_update_index_in_dim(fetched, received, active_index, 0)

    fetched = lax.fori_loop(
        0,
        active_count,
        fetch_one,
        jnp.zeros((active_count,) + stored_weight.shape[1:], jnp.bfloat16),
    )
    fetch_down = fetched[..., :model_width]
    fetch_up = fetched[..., model_width:]
    floats = tokens.astype(jnp.float32)
    normed = (
        floats
        * lax.rsqrt(jnp.mean(floats * floats, axis=-1, keepdims=True) + norm_eps)
        * input_norm_gain.astype(jnp.float32)
    ).astype(jnp.bfloat16)
    query_plain = jnp.dot(
        normed,
        lax.all_gather(query_weight, "req", axis=0, tiled=True),
        preferred_element_type=jnp.float32,
    )
    key_base = jnp.dot(
        normed,
        lax.all_gather(key_weight, "req", axis=0, tiled=True),
        preferred_element_type=jnp.float32,
    )
    value_plain = jnp.dot(
        normed,
        lax.all_gather(value_weight, "req", axis=0, tiled=True),
        preferred_element_type=jnp.float32,
    )
    request_total = request_adapters.shape[0]
    member = segment[:, None] == jnp.arange(request_total, dtype=jnp.int32)[None, :]
    token_adapter = jnp.sum(
        jnp.where(member, request_adapters[None, :], jnp.zeros_like(request_adapters)[None, :]),
        axis=1,
    )
    select = token_adapter[:, None] == jnp.arange(active_count, dtype=jnp.int32)[None, :]
    shrunk_all = lax.dot_general(
        normed,
        fetch_down.reshape(active_count * 2 * reduced_rows, model_width),
        (((1,), (1,)), ((), ())),
        preferred_element_type=jnp.float32,
    )
    shrunk_all = shrunk_all.reshape(row_total, active_count, 2, reduced_rows)
    shrunk = jnp.sum(
        jnp.where(select[:, :, None, None], shrunk_all, jnp.float32(0.0)), axis=1
    ).astype(jnp.bfloat16)
    spread = jnp.where(select[:, :, None, None], shrunk[:, None, :, :], jnp.zeros((), jnp.bfloat16))
    query_change = jnp.dot(
        spread[:, :, 0, :].reshape(row_total, active_count * reduced_rows),
        fetch_up[:, 0].reshape(active_count * reduced_rows, local_width),
        preferred_element_type=jnp.float32,
    )
    value_change = jnp.dot(
        spread[:, :, 1, :].reshape(row_total, active_count * reduced_rows),
        fetch_up[:, 1].reshape(active_count * reduced_rows, local_width),
        preferred_element_type=jnp.float32,
    )
    head_total = local_width // HEAD_WIDTH
    token_positions = positions_of(segment)
    query_per_head = apply_rotation(
        (query_plain + adapter_scale * query_change).reshape(row_total, head_total, HEAD_WIDTH),
        token_positions,
    ).astype(jnp.bfloat16)
    key_heads = apply_rotation(
        key_base.reshape(row_total, head_total, HEAD_WIDTH), token_positions
    ).astype(jnp.bfloat16)
    value_per_head = (
        (value_plain + adapter_scale * value_change)
        .astype(jnp.bfloat16)
        .reshape(row_total, head_total, HEAD_WIDTH)
    )
    attended = attend(query_per_head, key_heads, value_per_head, segment).reshape(
        row_total, local_width
    )
    partial_out = jnp.dot(
        attended,
        lax.all_gather(output_weight, "req", axis=1, tiled=True),
        preferred_element_type=jnp.float32,
    )
    summed = lax.psum_scatter(
        partial_out.astype(jnp.bfloat16), "tp", scatter_dimension=1, tiled=True
    ).astype(jnp.float32)
    share_width = summed.shape[1]
    residual_part = lax.dynamic_slice_in_dim(
        tokens, lax.axis_index("tp") * share_width, share_width, 1
    )
    return (summed + residual_part.astype(jnp.float32)).astype(jnp.bfloat16)


def solution(mesh):
    in_specs = (
        P("req", None),
        P("req", None),
        P("req", None),
        P(),
        P(),
        P(),
        P("req", "tp"),
        P("req", "tp"),
        P("req", "tp"),
        P("tp", "req"),
        P("req", None, None, None),
        P("req", None, None, "tp"),
    )
    out_specs = P("req", "tp")
    return jax.shard_map(local, mesh=mesh, in_specs=in_specs, out_specs=out_specs, check_vma=False)
```

profile of v0, /device:TPU:0, one launch (start us, length us, event | category | flops | bytes accessed | tf_op | source)
XLA Modules:
  0.0 1461.1 jit_solution(2238570392540167822)
XLA Ops:
  9.4 1.2 pad_maximum_fusion.12
  10.6 1205.2 %while.15 = (s32[]{:T(128)}, bf16[16,2,16,2560]{3,2,1,0:T(8,128)(2,1)}, s32[16]{0:T(128)S(1)}, bf16[2,2,16,2560]{3,2,1,0:T(8,128)(2,1)S(1)}, s32[]{:T(128)}, /*i...) while((s32[]{:T(128)}, bf16[16,2,16,2560]{3,2,1,0:T(8,128)(2,1)}, s32[16]{0:T(128)S(1)}, ...), condition=%wide.region_4.5_spmd, body=%wide.region_2.4_spmd.sunk | while | flops 163868 | bytes 1638832 | solution.py:87
  13.8 0.7 dynamic-slice_select_fusion.2
  14.5 72.8 %all-reduce.2.cloned.1.call-done = bf16[1,2,16,2560]{3,2,1,0:T(8,128)(2,1)} async-done(((bf16[1,2,16,2560]{3,2,1,0:T(8,128)(2,1)}), bf16[1,2,16,2560]{3,2,1,0:T(8,128)(2,1)}) %all-reduce.2.cloned.1.call-update) | async-done | bytes 163856 | tf_op jit(solution)/shard_map/while/body/eval_jaxpr/psum | solution.py:14
  87.3 1.6 constant_dynamic-update-slice_fusion.2
  92.1 0.7 dynamic-slice_select_fusion.2
  92.8 69.8 %all-reduce.2.cloned.1.call-done = bf16[1,2,16,2560]{3,2,1,0:T(8,128)(2,1)} async-done(((bf16[1,2,16,2560]{3,2,1,0:T(8,128)(2,1)}), bf16[1,2,16,2560]{3,2,1,0:T(8,128)(2,1)}) %all-reduce.2.cloned.1.call-update) | async-done | bytes 163856 | tf_op jit(solution)/shard_map/while/body/eval_jaxpr/psum | solution.py:14
  162.6 1.6 constant_dynamic-update-slice_fusion.2
  167.4 0.7 dynamic-slice_select_fusion.2
  168.1 69.8 %all-reduce.2.cloned.1.call-done = bf16[1,2,16,2560]{3,2,1,0:T(8,128)(2,1)} async-done(((bf16[1,2,16,2560]{3,2,1,0:T(8,128)(2,1)}), bf16[1,2,16,2560]{3,2,1,0:T(8,128)(2,1)}) %all-reduce.2.cloned.1.call-update) | async-done | bytes 163856 | tf_op jit(solution)/shard_map/while/body/eval_jaxpr/psum | solution.py:14
  237.8 1.6 constant_dynamic-update-slice_fusion.2
  242.6 0.7 dynamic-slice_select_fusion.2
  243.3 69.5 %all-reduce.2.cloned.1.call-done = bf16[1,2,16,2560]{3,2,1,0:T(8,128)(2,1)} async-done(((bf16[1,2,16,2560]{3,2,1,0:T(8,128)(2,1)}), bf16[1,2,16,2560]{3,2,1,0:T(8,128)(2,1)}) %all-reduce.2.cloned.1.call-update) | async-done | bytes 163856 | tf_op jit(solution)/shard_map/while/body/eval_jaxpr/psum | solution.py:14
  312.8 1.6 constant_dynamic-update-slice_fusion.2
  317.6 0.7 dynamic-slice_select_fusion.2
  318.3 69.5 %all-reduce.2.cloned.1.call-done = bf16[1,2,16,2560]{3,2,1,0:T(8,128)(2,1)} async-done(((bf16[1,2,16,2560]{3,2,1,0:T(8,128)(2,1)}), bf16[1,2,16,2560]{3,2,1,0:T(8,128)(2,1)}) %all-reduce.2.cloned.1.call-update) | async-done | bytes 163856 | tf_op jit(solution)/shard_map/while/body/eval_jaxpr/psum | solution.py:14
  387.8 1.6 constant_dynamic-update-slice_fusion.2
  392.6 0.7 dynamic-slice_select_fusion.2
  393.3 69.5 %all-reduce.2.cloned.1.call-done = bf16[1,2,16,2560]{3,2,1,0:T(8,128)(2,1)} async-done(((bf16[1,2,16,2560]{3,2,1,0:T(8,128)(2,1)}), bf16[1,2,16,2560]{3,2,1,0:T(8,128)(2,1)}) %all-reduce.2.cloned.1.call-update) | async-done | bytes 163856 | tf_op jit(solution)/shard_map/while/body/eval_jaxpr/psum | solution.py:14
  462.8 1.6 constant_dynamic-update-slice_fusion.2
  467.6 0.7 dynamic-slice_select_fusion.2
  468.3 69.8 %all-reduce.2.cloned.1.call-done = bf16[1,2,16,2560]{3,2,1,0:T(8,128)(2,1)} async-done(((bf16[1,2,16,2560]{3,2,1,0:T(8,128)(2,1)}), bf16[1,2,16,2560]{3,2,1,0:T(8,128)(2,1)}) %all-reduce.2.cloned.1.call-update) | async-done | bytes 163856 | tf_op jit(solution)/shard_map/while/body/eval_jaxpr/psum | solution.py:14
  538.1 1.6 constant_dynamic-update-slice_fusion.2
  542.9 0.7 dynamic-slice_select_fusion.2
  543.6 69.8 %all-reduce.2.cloned.1.call-done = bf16[1,2,16,2560]{3,2,1,0:T(8,128)(2,1)} async-done(((bf16[1,2,16,2560]{3,2,1,0:T(8,128)(2,1)}), bf16[1,2,16,2560]{3,2,1,0:T(8,128)(2,1)}) %all-reduce.2.cloned.1.call-update) | async-done | bytes 163856 | tf_op jit(solution)/shard_map/while/body/eval_jaxpr/psum | solution.py:14
  613.4 1.6 constant_dynamic-update-slice_fusion.2
  618.2 0.7 dynamic-slice_select_fusion.2
  618.9 69.8 %all-reduce.2.cloned.1.call-done = bf16[1,2,16,2560]{3,2,1,0:T(8,128)(2,1)} async-done(((bf16[1,2,16,2560]{3,2,1,0:T(8,128)(2,1)}), bf16[1,2,16,2560]{3,2,1,0:T(8,128)(2,1)}) %all-reduce.2.cloned.1.call-update) | async-done | bytes 163856 | tf_op jit(solution)/shard_map/while/body/eval_jaxpr/psum | solution.py:14
  688.7 1.6 constant_dynamic-update-slice_fusion.2
  693.5 0.7 dynamic-slice_select_fusion.2
  694.2 69.5 %all-reduce.2.cloned.1.call-done = bf16[1,2,16,2560]{3,2,1,0:T(8,128)(2,1)} async-done(((bf16[1,2,16,2560]{3,2,1,0:T(8,128)(2,1)}), bf16[1,2,16,2560]{3,2,1,0:T(8,128)(2,1)}) %all-reduce.2.cloned.1.call-update) | async-done | bytes 163856 | tf_op jit(solution)/shard_map/while/body/eval_jaxpr/psum | solution.py:14
  763.6 1.6 constant_dynamic-update-slice_fusion.2
  768.4 0.7 dynamic-slice_select_fusion.2
  769.1 69.8 %all-reduce.2.cloned.1.call-done = bf16[1,2,16,2560]{3,2,1,0:T(8,128)(2,1)} async-done(((bf16[1,2,16,2560]{3,2,1,0:T(8,128)(2,1)}), bf16[1,2,16,2560]{3,2,1,0:T(8,128)(2,1)}) %all-reduce.2.cloned.1.call-update) | async-done | bytes 163856 | tf_op jit(solution)/shard_map/while/body/eval_jaxpr/psum | solution.py:14
  838.9 1.6 constant_dynamic-update-slice_fusion.2
  843.7 0.7 dynamic-slice_select_fusion.2
  844.4 69.5 %all-reduce.2.cloned.1.call-done = bf16[1,2,16,2560]{3,2,1,0:T(8,128)(2,1)} async-done(((bf16[1,2,16,2560]{3,2,1,0:T(8,128)(2,1)}), bf16[1,2,16,2560]{3,2,1,0:T(8,128)(2,1)}) %all-reduce.2.cloned.1.call-update) | async-done | bytes 163856 | tf_op jit(solution)/shard_map/while/body/eval_jaxpr/psum | solution.py:14
  913.9 1.6 constant_dynamic-update-slice_fusion.2
  918.7 0.7 dynamic-slice_select_fusion.2
  919.4 69.8 %all-reduce.2.cloned.1.call-done = bf16[1,2,16,2560]{3,2,1,0:T(8,128)(2,1)} async-done(((bf16[1,2,16,2560]{3,2,1,0:T(8,128)(2,1)}), bf16[1,2,16,2560]{3,2,1,0:T(8,128)(2,1)}) %all-reduce.2.cloned.1.call-update) | async-done | bytes 163856 | tf_op jit(solution)/shard_map/while/body/eval_jaxpr/psum | solution.py:14
  989.2 1.6 constant_dynamic-update-slice_fusion.2
  994.7 69.5 %all-reduce.2.cloned.1.call-done = bf16[1,2,16,2560]{3,2,1,0:T(8,128)(2,1)} async-done(((bf16[1,2,16,2560]{3,2,1,0:T(8,128)(2,1)}), bf16[1,2,16,2560]{3,2,1,0:T(8,128)(2,1)}) %all-reduce.2.cloned.1.call-update) | async-done | bytes 163856 | tf_op jit(solution)/shard_map/while/body/eval_jaxpr/psum | solution.py:14
  1064.2 1.6 constant_dynamic-update-slice_fusion.2
  1069.7 69.5 %all-reduce.2.cloned.1.call-done = bf16[1,2,16,2560]{3,2,1,0:T(8,128)(2,1)} async-done(((bf16[1,2,16,2560]{3,2,1,0:T(8,128)(2,1)}), bf16[1,2,16,2560]{3,2,1,0:T(8,128)(2,1)}) %all-reduce.2.cloned.1.call-update) | async-done | bytes 163856 | tf_op jit(solution)/shard_map/while/body/eval_jaxpr/psum | solution.py:14
  1139.1 1.6 constant_dynamic-update-slice_fusion.2
  1144.6 69.5 %all-reduce.2.cloned.1.call-done = bf16[1,2,16,2560]{3,2,1,0:T(8,128)(2,1)} async-done(((bf16[1,2,16,2560]{3,2,1,0:T(8,128)(2,1)}), bf16[1,2,16,2560]{3,2,1,0:T(8,128)(2,1)}) %all-reduce.2.cloned.1.call-update) | async-done | bytes 163856 | tf_op jit(solution)/shard_map/while/body/eval_jaxpr/psum | solution.py:14
  1214.1 1.6 constant_dynamic-update-slice_fusion.2
  1218.9 0.9 fusion.28
  1219.9 3.0 fusion.23
  1223.9 43.4 %all-gather.5.cloned.1.call-done = bf16[2048,512]{1,0:T(8,128)(2,1)} async-done(((bf16[256,512]{1,0:T(8,128)(2,1)}), bf16[2048,512]{1,0:T(8,128)(2,1)}) %all-gather.5.cloned.1.call-update) | async-done | bytes 2097168 | tf_op jit(solution)/shard_map/all_gather | solution.py:113
  1267.3 3.0 fusion.44
  1270.4 2.1 fusion.22
  1272.5 44.6 %all-gather.7.cloned.1.call-done = bf16[2048,512]{1,0:T(8,128)(2,1)} async-done(((bf16[256,512]{1,0:T(8,128)(2,1)}), bf16[2048,512]{1,0:T(8,128)(2,1)}) %all-gather.7.cloned.1.call-update) | async-done | bytes 2097168 | tf_op jit(solution)/shard_map/all_gather | solution.py:103
  1317.1 3.1 fusion.41
  1320.2 1.3 fusion.20
  1321.5 45.3 %all-gather.9.cloned.1.call-done = bf16[2048,512]{1,0:T(8,128)(2,1)} async-done(((bf16[256,512]{1,0:T(8,128)(2,1)}), bf16[2048,512]{1,0:T(8,128)(2,1)}) %all-gather.9.cloned.1.call-update) | async-done | bytes 2097168 | tf_op jit(solution)/shard_map/all_gather | solution.py:108
  1366.8 3.0 fusion.39
  1369.8 1.3 subtract_convert_fusion.1
  1371.1 8.1 fusion.46
  1379.2 4.3 fusion.21
  1383.5 34.4 %all-gather.11.cloned.1.call-done = bf16[512,2048]{1,0:T(8,128)(2,1)} async-done(((bf16[512,256]{1,0:T(8,128)(2,1)}), bf16[512,2048]{1,0:T(8,128)(2,1)}) %all-gather.11.cloned.1.call-update) | async-done | bytes 2097168 | tf_op jit(solution)/shard_map/all_gather | solution.py:163
  1417.9 4.2 convolution_convert_fusion
  1422.2 29.6 %reduce-scatter.2.cloned.1.call-done = bf16[512,512]{1,0:T(8,128)(2,1)} async-done(((bf16[512,2048]{1,0:T(8,128)(2,1)}), bf16[512,512]{1,0:T(8,128)(2,1)}) %reduce-scatter.2.cloned.1.call-update) | async-done | bytes 524304 | tf_op jit(solution)/shard_map/reduce_scatter | solution.py:166
  1451.8 2.0 add_convert_fusion
  (97 shorter events, 18.0 us)
Async XLA Ops:
  7.4 0.7 copy-start
  9.4 1208.9 %copy-start.1 = (bf16[512,2048]{1,0:T(8,128)(2,1)S(1)}, bf16[512,2048]{1,0:T(8,128)(2,1)}, u32[]{:S(2)}) copy-start(bf16[512,2048]{1,0:T(8,128)(2,1)} %param.14) | copy-start | bytes 6291460
  10.5 1207.7 %copy-start.6 = (bf16[2048]{0:T(1024)(128)(2,1)S(1)}, bf16[2048]{0:T(1024)(128)(2,1)}, u32[]{:S(2)}) copy-start(bf16[2048]{0:T(1024)(128)(2,1)} %param.19) | copy-start | bytes 12292
  10.6 76.7 %all-reduce.2.cloned.1.call-start = ((), (), s32[]{:S(2)}) async-start(), calls=%async_computation.6 | async-start | bytes 327680 | tf_op jit(solution)/shard_map/while/body/eval_jaxpr/psum | solution.py:14
  88.9 73.7 %all-reduce.2.cloned.1.call-start = ((), (), s32[]{:S(2)}) async-start(), calls=%async_computation.6 | async-start | bytes 327680 | tf_op jit(solution)/shard_map/while/body/eval_jaxpr/psum | solution.py:14
  164.2 73.7 %all-reduce.2.cloned.1.call-start = ((), (), s32[]{:S(2)}) async-start(), calls=%async_computation.6 | async-start | bytes 327680 | tf_op jit(solution)/shard_map/while/body/eval_jaxpr/psum | solution.py:14
  239.4 73.4 %all-reduce.2.cloned.1.call-start = ((), (), s32[]{:S(2)}) async-start(), calls=%async_computation.6 | async-start | bytes 327680 | tf_op jit(solution)/shard_map/while/body/eval_jaxpr/psum | solution.py:14
  314.4 73.4 %all-reduce.2.cloned.1.call-start = ((), (), s32[]{:S(2)}) async-start(), calls=%async_computation.6 | async-start | bytes 327680 | tf_op jit(solution)/shard_map/while/body/eval_jaxpr/psum | solution.py:14
  389.4 73.4 %all-reduce.2.cloned.1.call-start = ((), (), s32[]{:S(2)}) async-start(), calls=%async_computation.6 | async-start | bytes 327680 | tf_op jit(solution)/shard_map/while/body/eval_jaxpr/psum | solution.py:14
  464.4 73.7 %all-reduce.2.cloned.1.call-start = ((), (), s32[]{:S(2)}) async-start(), calls=%async_computation.6 | async-start | bytes 327680 | tf_op jit(solution)/shard_map/while/body/eval_jaxpr/psum | solution.py:14
  539.7 73.7 %all-reduce.2.cloned.1.call-start = ((), (), s32[]{:S(2)}) async-start(), calls=%async_computation.6 | async-start | bytes 327680 | tf_op jit(solution)/shard_map/while/body/eval_jaxpr/psum | solution.py:14
  615.0 73.7 %all-reduce.2.cloned.1.call-start = ((), (), s32[]{:S(2)}) async-start(), calls=%async_computation.6 | async-start | bytes 327680 | tf_op jit(solution)/shard_map/while/body/eval_jaxpr/psum | solution.py:14
  690.2 73.4 %all-reduce.2.cloned.1.call-start = ((), (), s32[]{:S(2)}) async-start(), calls=%async_computation.6 | async-start | bytes 327680 | tf_op jit(solution)/shard_map/while/body/eval_jaxpr/psum | solution.py:14
  765.2 73.7 %all-reduce.2.cloned.1.call-start = ((), (), s32[]{:S(2)}) async-start(), calls=%async_computation.6 | async-start | bytes 327680 | tf_op jit(solution)/shard_map/while/body/eval_jaxpr/psum | solution.py:14
  840.5 73.4 %all-reduce.2.cloned.1.call-start = ((), (), s32[]{:S(2)}) async-start(), calls=%async_computation.6 | async-start | bytes 327680 | tf_op jit(solution)/shard_map/while/body/eval_jaxpr/psum | solution.py:14
  915.5 73.7 %all-reduce.2.cloned.1.call-start = ((), (), s32[]{:S(2)}) async-start(), calls=%async_computation.6 | async-start | bytes 327680 | tf_op jit(solution)/shard_map/while/body/eval_jaxpr/psum | solution.py:14
  990.8 73.4 %all-reduce.2.cloned.1.call-start = ((), (), s32[]{:S(2)}) async-start(), calls=%async_computation.6 | async-start | bytes 327680 | tf_op jit(solution)/shard_map/while/body/eval_jaxpr/psum | solution.py:14
  1065.8 73.4 %all-reduce.2.cloned.1.call-start = ((), (), s32[]{:S(2)}) async-start(), calls=%async_computation.6 | async-start | bytes 327680 | tf_op jit(solution)/shard_map/while/body/eval_jaxpr/psum | solution.py:14
  1140.7 73.4 %all-reduce.2.cloned.1.call-start = ((), (), s32[]{:S(2)}) async-start(), calls=%async_computation.6 | async-start | bytes 327680 | tf_op jit(solution)/shard_map/while/body/eval_jaxpr/psum | solution.py:14
  1215.7 3.1 copy-start.5
  1215.7 4.1 copy-start.7
  1215.7 51.6 %all-gather.5.cloned.1.call-start = ((), (), s32[]{:S(2)}) async-start(), calls=%async_computation.1 | async-start | bytes 2359296 | tf_op jit(solution)/shard_map/all_gather | solution.py:113
  1216.3 100.8 %all-gather.7.cloned.1.call-start = ((), (), s32[]{:S(2)}) async-start(), calls=%async_computation.2 | async-start | bytes 2359296 | tf_op jit(solution)/shard_map/all_gather | solution.py:103
  1216.9 149.9 %all-gather.9.cloned.1.call-start = ((), (), s32[]{:S(2)}) async-start(), calls=%async_computation.3 | async-start | bytes 2359296 | tf_op jit(solution)/shard_map/all_gather | solution.py:108
  1217.5 200.4 %all-gather.11.cloned.1.call-start = ((), (), s32[]{:S(2)}) async-start(), calls=%async_computation.4 | async-start | bytes 2359296 | tf_op jit(solution)/shard_map/all_gather | solution.py:163
  1218.2 233.6 %reduce-scatter.2.cloned.1.call-start = ((), (), s32[]{:S(2)}) async-start(), calls=%async_computation.5 | async-start | bytes 2621440 | tf_op jit(solution)/shard_map/reduce_scatter | solution.py:166
  1222.9 47.4 %copy-start.2 = (bf16[512,16,2,16]{0,3,2,1:T(8,128)(2,1)}, bf16[512,16,2,16]{0,3,2,1:T(8,128)(2,1)S(1)}, u32[]{:S(2)}) copy-start(bf16[512,16,2,16]{0,3,2,1:T(8,128)(2,1)S(1)} %broadcast_select_fusion) | copy-start | bytes 1572868
  1317.0 3.1 copy-start.3
  1371.1 8.1 copy-start.4
Sparse Core Ops, SparseCore 0:
  15.1 72.1 all-reduce.1
  93.4 69.1 all-reduce.1
  168.7 69.1 all-reduce.1
  243.6 69.1 all-reduce.1
  318.6 69.1 all-reduce.1
  393.6 69.1 all-reduce.1
  468.9 69.1 all-reduce.1
  544.2 69.1 all-reduce.1
  619.5 69.1 all-reduce.1
  694.5 69.1 all-reduce.1
  769.7 69.1 all-reduce.1
  844.7 69.1 all-reduce.1
  920.0 69.1 all-reduce.1
  995.0 69.1 all-reduce.1
  1070.0 69.1 all-reduce.1
  1144.9 69.1 all-reduce.1
Sparse Core Ops, SparseCore 1:
  1218.3 49.0 all-gather.4
  1269.3 47.7 all-gather.6
  1319.0 47.7 all-gather.8
  1368.8 49.0 all-gather.10
  1422.3 29.5 reduce-scatter.1
where the time goes:
time: 1460 us
  waiting for transfers between devices  1320 us (90%)
  loops' own time  42.1 us (3%)
  local copies, waits for them, and re-layouts  35.6 us (2%)
  matrix products  32.2 us (2%)
  other arithmetic  19.2 us (1%)
  between operations  14.9 us (1%)
    psum x16, waiting for transfers between devices, spread_2(): return lax.psum(jnp.where(mine, value, jnp.zeros_like(value)), axis)  1120 us
    all_gather x1, waiting for transfers between devices, local(): lax.all_gather(key_weight, 'req', axis=0, tiled=True)  45.3 us
    all_gather x1, waiting for transfers between devices, local(): lax.all_gather(query_weight, 'req', axis=0, tiled=True)  44.6 us
    all_gather x1, waiting for transfers between devices, local(): lax.all_gather(value_weight, 'req', axis=0, tiled=True)  43.4 us
    another operation x1, loops' own time, local(): lax.fori_loop(0, active_count, fetch_one, jnp.zeros((active_count,) + sto...  42.1 us
    all_gather x1, waiting for transfers between devices, local(): lax.all_gather(output_weight, 'req', axis=1, tiled=True)  34.4 us
    reduce_scatter x1, waiting for transfers between devices, local(): lax.psum_scatter(partial_out.astype(jnp.bfloat16), 'tp', scatter_dimensio...  29.6 us
  transfers between devices with their start and end apart: 21, of which 21 were waited for; matrix products, arithmetic and copies ran while one was open for 2% of the time, Pallas kernels for 0%

commit v1 on v0

--- a/solution.py
+++ b/solution.py
@@ -7,6 +7,16 @@
 norm_eps = 1e-05
 rope_base = 130000.0
 adapter_scale = 2.0
+
+
+def ring_gather(x, axis, dim):
+    ways, here, step = (lax.axis_size(axis), lax.axis_index(axis), x.shape[dim])
+    shape = [n * ways if d == dim else n for d, n in enumerate(x.shape)]
+    full = lax.dynamic_update_slice_in_dim(jnp.zeros(shape, x.dtype), x, here * step, axis=dim)
+    for far in range(1, ways):
+        x = lax.ppermute(x, axis, [(d, (d + 1) % ways) for d in range(ways)])
+        full = lax.dynamic_update_slice_in_dim(full, x, (here - far) % ways * step, axis=dim)
+    return full
 
 
 def spread_2(value, axis, root):
@@ -104,9 +114,7 @@
         preferred_element_type=jnp.float32,
     )
     key_base = jnp.dot(
-        normed,
-        lax.all_gather(key_weight, "req", axis=0, tiled=True),
-        preferred_element_type=jnp.float32,
+        normed, ring_gather(key_weight, "req", 0), preferred_element_type=jnp.float32
     )
     value_plain = jnp.dot(
         normed,

time: 1460 us -> 1430 us (0.979)
  waiting for transfers between devices: 1320 us -> 1270 us
    ppermute x0 -> x7, waiting for transfers between devices: none -> 72.9 us  [ring_gather(): x = lax.ppermute(x, axis, [(d, (d + 1) % ways) for d in range(ways)])]
    all_gather x1 -> x0, waiting for transfers between devices: 45.3 us -> none  [local(): lax.all_gather(key_weight, 'req', axis=0, tiled=True)]
    all_gather x1, waiting for transfers between devices: 43.4 us -> 0.01 us  [local(): lax.all_gather(value_weight, 'req', axis=0, tiled=True)]
    all_gather x1, waiting for transfers between devices: 44.6 us -> 16.6 us  [local(): lax.all_gather(query_weight, 'req', axis=0, tiled=True)]
  transfers between devices with their start and end apart: 21 -> 27, of which waited for: 21 -> 26; matrix products, arithmetic and copies ran while one was open for 2% -> 3% of each run, Pallas kernels for 0% -> 0%
where the time goes in v1:
time: 1430 us
  waiting for transfers between devices  1270 us (89%)
  local copies, waits for them, and re-layouts  44.7 us (3%)
  loops' own time  42.1 us (3%)
  matrix products  32.2 us (2%)
  other arithmetic  19.6 us (1%)
  between operations  15 us (1%)
    psum x16, waiting for transfers between devices, spread_2(): return lax.psum(jnp.where(mine, value, jnp.zeros_like(value)), axis)  1120 us
    ppermute x7, waiting for transfers between devices, ring_gather(): x = lax.ppermute(x, axis, [(d, (d + 1) % ways) for d in range(ways)])  72.9 us
    another operation x1, loops' own time, local(): lax.fori_loop(0, active_count, fetch_one, jnp.zeros((active_count,) + sto...  42.1 us
    all_gather x1, waiting for transfers between devices, local(): lax.all_gather(output_weight, 'req', axis=1, tiled=True)  33.2 us
    reduce_scatter x1, waiting for transfers between devices, local(): lax.psum_scatter(partial_out.astype(jnp.bfloat16), 'tp', scatter_dimensio...  29.6 us
  transfers between devices with their start and end apart: 27, of which 26 were waited for; matrix products, arithmetic and copies ran while one was open for 3% of the time, Pallas kernels for 0%

profile of v1, /device:TPU:0, one launch (start us, length us, event | category | flops | bytes accessed | tf_op | source)
XLA Modules:
  0.0 1425.8 jit_solution(9688842935571006525)
XLA Ops:
  9.4 1.2 pad_maximum_fusion.12
  10.6 1205.2 %while.15 = (s32[]{:T(128)}, bf16[16,2,16,2560]{3,2,1,0:T(8,128)(2,1)}, s32[16]{0:T(128)S(1)}, bf16[2,2,16,2560]{3,2,1,0:T(8,128)(2,1)S(1)}, s32[]{:T(128)}, /*i...) while((s32[]{:T(128)}, bf16[16,2,16,2560]{3,2,1,0:T(8,128)(2,1)}, s32[16]{0:T(128)S(1)}, ...), condition=%wide.region_4.5_spmd, body=%wide.region_2.4_spmd.sunk | while | flops 163868 | bytes 1638832 | solution.py:97
  14.5 72.8 %all-reduce.2.cloned.1.call-done = bf16[1,2,16,2560]{3,2,1,0:T(8,128)(2,1)} async-done(((bf16[1,2,16,2560]{3,2,1,0:T(8,128)(2,1)}), bf16[1,2,16,2560]{3,2,1,0:T(8,128)(2,1)}) %all-reduce.2.cloned.1.call-update) | async-done | bytes 163856 | tf_op jit(solution)/shard_map/while/body/eval_jaxpr/psum | solution.py:24
  87.3 1.6 constant_dynamic-update-slice_fusion.10
  92.8 69.8 %all-reduce.2.cloned.1.call-done = bf16[1,2,16,2560]{3,2,1,0:T(8,128)(2,1)} async-done(((bf16[1,2,16,2560]{3,2,1,0:T(8,128)(2,1)}), bf16[1,2,16,2560]{3,2,1,0:T(8,128)(2,1)}) %all-reduce.2.cloned.1.call-update) | async-done | bytes 163856 | tf_op jit(solution)/shard_map/while/body/eval_jaxpr/psum | solution.py:24
  162.6 1.6 constant_dynamic-update-slice_fusion.10
  168.1 69.8 %all-reduce.2.cloned.1.call-done = bf16[1,2,16,2560]{3,2,1,0:T(8,128)(2,1)} async-done(((bf16[1,2,16,2560]{3,2,1,0:T(8,128)(2,1)}), bf16[1,2,16,2560]{3,2,1,0:T(8,128)(2,1)}) %all-reduce.2.cloned.1.call-update) | async-done | bytes 163856 | tf_op jit(solution)/shard_map/while/body/eval_jaxpr/psum | solution.py:24
  237.9 1.6 constant_dynamic-update-slice_fusion.10
  243.4 69.5 %all-reduce.2.cloned.1.call-done = bf16[1,2,16,2560]{3,2,1,0:T(8,128)(2,1)} async-done(((bf16[1,2,16,2560]{3,2,1,0:T(8,128)(2,1)}), bf16[1,2,16,2560]{3,2,1,0:T(8,128)(2,1)}) %all-reduce.2.cloned.1.call-update) | async-done | bytes 163856 | tf_op jit(solution)/shard_map/while/body/eval_jaxpr/psum | solution.py:24
  312.9 1.6 constant_dynamic-update-slice_fusion.10
  318.4 69.5 %all-reduce.2.cloned.1.call-done = bf16[1,2,16,2560]{3,2,1,0:T(8,128)(2,1)} async-done(((bf16[1,2,16,2560]{3,2,1,0:T(8,128)(2,1)}), bf16[1,2,16,2560]{3,2,1,0:T(8,128)(2,1)}) %all-reduce.2.cloned.1.call-update) | async-done | bytes 163856 | tf_op jit(solution)/shard_map/while/body/eval_jaxpr/psum | solution.py:24
  387.8 1.6 constant_dynamic-update-slice_fusion.10
  393.3 69.5 %all-reduce.2.cloned.1.call-done = bf16[1,2,16,2560]{3,2,1,0:T(8,128)(2,1)} async-done(((bf16[1,2,16,2560]{3,2,1,0:T(8,128)(2,1)}), bf16[1,2,16,2560]{3,2,1,0:T(8,128)(2,1)}) %all-reduce.2.cloned.1.call-update) | async-done | bytes 163856 | tf_op jit(solution)/shard_map/while/body/eval_jaxpr/psum | solution.py:24
  462.8 1.6 constant_dynamic-update-slice_fusion.10
  468.3 69.8 %all-reduce.2.cloned.1.call-done = bf16[1,2,16,2560]{3,2,1,0:T(8,128)(2,1)} async-done(((bf16[1,2,16,2560]{3,2,1,0:T(8,128)(2,1)}), bf16[1,2,16,2560]{3,2,1,0:T(8,128)(2,1)}) %all-reduce.2.cloned.1.call-update) | async-done | bytes 163856 | tf_op jit(solution)/shard_map/while/body/eval_jaxpr/psum | solution.py:24
  538.1 1.6 constant_dynamic-update-slice_fusion.10
  543.6 69.8 %all-reduce.2.cloned.1.call-done = bf16[1,2,16,2560]{3,2,1,0:T(8,128)(2,1)} async-done(((bf16[1,2,16,2560]{3,2,1,0:T(8,128)(2,1)}), bf16[1,2,16,2560]{3,2,1,0:T(8,128)(2,1)}) %all-reduce.2.cloned.1.call-update) | async-done | bytes 163856 | tf_op jit(solution)/shard_map/while/body/eval_jaxpr/psum | solution.py:24
  613.4 1.6 constant_dynamic-update-slice_fusion.10
  618.9 69.8 %all-reduce.2.cloned.1.call-done = bf16[1,2,16,2560]{3,2,1,0:T(8,128)(2,1)} async-done(((bf16[1,2,16,2560]{3,2,1,0:T(8,128)(2,1)}), bf16[1,2,16,2560]{3,2,1,0:T(8,128)(2,1)}) %all-reduce.2.cloned.1.call-update) | async-done | bytes 163856 | tf_op jit(solution)/shard_map/while/body/eval_jaxpr/psum | solution.py:24
  688.7 1.6 constant_dynamic-update-slice_fusion.10
  694.2 69.5 %all-reduce.2.cloned.1.call-done = bf16[1,2,16,2560]{3,2,1,0:T(8,128)(2,1)} async-done(((bf16[1,2,16,2560]{3,2,1,0:T(8,128)(2,1)}), bf16[1,2,16,2560]{3,2,1,0:T(8,128)(2,1)}) %all-reduce.2.cloned.1.call-update) | async-done | bytes 163856 | tf_op jit(solution)/shard_map/while/body/eval_jaxpr/psum | solution.py:24
  763.7 1.6 constant_dynamic-update-slice_fusion.10
  769.2 69.8 %all-reduce.2.cloned.1.call-done = bf16[1,2,16,2560]{3,2,1,0:T(8,128)(2,1)} async-done(((bf16[1,2,16,2560]{3,2,1,0:T(8,128)(2,1)}), bf16[1,2,16,2560]{3,2,1,0:T(8,128)(2,1)}) %all-reduce.2.cloned.1.call-update) | async-done | bytes 163856 | tf_op jit(solution)/shard_map/while/body/eval_jaxpr/psum | solution.py:24
  838.9 1.6 constant_dynamic-update-slice_fusion.10
  844.4 69.5 %all-reduce.2.cloned.1.call-done = bf16[1,2,16,2560]{3,2,1,0:T(8,128)(2,1)} async-done(((bf16[1,2,16,2560]{3,2,1,0:T(8,128)(2,1)}), bf16[1,2,16,2560]{3,2,1,0:T(8,128)(2,1)}) %all-reduce.2.cloned.1.call-update) | async-done | bytes 163856 | tf_op jit(solution)/shard_map/while/body/eval_jaxpr/psum | solution.py:24
  913.9 1.6 constant_dynamic-update-slice_fusion.10
  919.4 69.8 %all-reduce.2.cloned.1.call-done = bf16[1,2,16,2560]{3,2,1,0:T(8,128)(2,1)} async-done(((bf16[1,2,16,2560]{3,2,1,0:T(8,128)(2,1)}), bf16[1,2,16,2560]{3,2,1,0:T(8,128)(2,1)}) %all-reduce.2.cloned.1.call-update) | async-done | bytes 163856 | tf_op jit(solution)/shard_map/while/body/eval_jaxpr/psum | solution.py:24
  989.2 1.6 constant_dynamic-update-slice_fusion.10
  994.7 69.5 %all-reduce.2.cloned.1.call-done = bf16[1,2,16,2560]{3,2,1,0:T(8,128)(2,1)} async-done(((bf16[1,2,16,2560]{3,2,1,0:T(8,128)(2,1)}), bf16[1,2,16,2560]{3,2,1,0:T(8,128)(2,1)}) %all-reduce.2.cloned.1.call-update) | async-done | bytes 163856 | tf_op jit(solution)/shard_map/while/body/eval_jaxpr/psum | solution.py:24
  1064.2 1.6 constant_dynamic-update-slice_fusion.10
  1069.7 69.5 %all-reduce.2.cloned.1.call-done = bf16[1,2,16,2560]{3,2,1,0:T(8,128)(2,1)} async-done(((bf16[1,2,16,2560]{3,2,1,0:T(8,128)(2,1)}), bf16[1,2,16,2560]{3,2,1,0:T(8,128)(2,1)}) %all-reduce.2.cloned.1.call-update) | async-done | bytes 163856 | tf_op jit(solution)/shard_map/while/body/eval_jaxpr/psum | solution.py:24
  1139.2 1.6 constant_dynamic-update-slice_fusion.10
  1144.6 69.5 %all-reduce.2.cloned.1.call-done = bf16[1,2,16,2560]{3,2,1,0:T(8,128)(2,1)} async-done(((bf16[1,2,16,2560]{3,2,1,0:T(8,128)(2,1)}), bf16[1,2,16,2560]{3,2,1,0:T(8,128)(2,1)}) %all-reduce.2.cloned.1.call-update) | async-done | bytes 163856 | tf_op jit(solution)/shard_map/while/body/eval_jaxpr/psum | solution.py:24
  1214.1 1.6 constant_dynamic-update-slice_fusion.10
  1217.0 1.3 collective-permute-start
  1219.0 3.0 fusion.23
  1221.9 4.1 collective-permute-done
  1226.8 14.9 %collective-permute-done.1 = bf16[256,512]{1,0:T(8,128)(2,1)S(1)} collective-permute-done((bf16[256,512]{1,0:T(8,128)(2,1)S(1)}, bf16[256,512]{1,0:T(8,128)(2,1)S(1)}, u32[]{:S(2)}, u32[]{:S(2)}) %collective-permute-start.1) | collective-permute-done | bytes 262176 | tf_op jit(solution)/shard_map/ppermute | solution.py:17
  1241.8 9.0 collective-permute-done.2
  1250.8 0.9 multiply_cosine_fusion
  1251.8 0.9 fusion.28
  1252.7 14.8 %collective-permute-done.3 = bf16[256,512]{1,0:T(8,128)(2,1)} collective-permute-done((bf16[256,512]{1,0:T(8,128)(2,1)S(1)}, bf16[256,512]{1,0:T(8,128)(2,1)}, u32[]{:S(2)}, u32[]{:S(2)}) %collective-permute-start.3) | collective-permute-done | bytes 262176 | tf_op jit(solution)/shard_map/ppermute | solution.py:17
  1267.5 1.4 broadcast_in_dim.123
  1268.9 0.7 constant_dynamic-update-slice_fusion.8
  1269.7 13.0 collective-permute-done.4
  1284.9 9.0 collective-permute-done.5
  1293.9 1.7 constant_dynamic-update-slice_fusion.4
  1295.6 1.7 constant_dynamic-update-slice_fusion.3
  1297.2 0.7 constant_dynamic-update-slice_fusion.2
  1298.0 8.0 collective-permute-done.6
  1306.0 0.7 constant_dynamic-update-slice_fusion.1
  1306.7 4.0 fusion.39
  1310.7 3.0 fusion.44
  1313.7 1.3 fusion.22
  1315.1 16.6 %all-gather.6.cloned.1.call-done = bf16[2048,512]{1,0:T(8,128)(2,1)} async-done(((bf16[256,512]{1,0:T(8,128)(2,1)}), bf16[2048,512]{1,0:T(8,128)(2,1)}) %all-gather.6.cloned.1.call-update) | async-done | bytes 2097168 | tf_op jit(solution)/shard_map/all_gather | solution.py:113
  1331.6 3.0 fusion.41
  1334.7 1.4 fusion.20
  1336.1 1.1 subtract_convert_fusion.1
  1337.2 7.9 fusion.46
  1345.1 4.3 fusion.21
  1349.4 33.2 %all-gather.8.cloned.1.call-done = bf16[512,2048]{1,0:T(8,128)(2,1)} async-done(((bf16[512,256]{1,0:T(8,128)(2,1)}), bf16[512,2048]{1,0:T(8,128)(2,1)}) %all-gather.8.cloned.1.call-update) | async-done | bytes 2097168 | tf_op jit(solution)/shard_map/all_gather | solution.py:171
  1382.6 4.2 convolution_convert_fusion
  1386.8 29.6 %reduce-scatter.2.cloned.1.call-done = bf16[512,512]{1,0:T(8,128)(2,1)} async-done(((bf16[512,2048]{1,0:T(8,128)(2,1)}), bf16[512,512]{1,0:T(8,128)(2,1)}) %reduce-scatter.2.cloned.1.call-update) | async-done | bytes 524304 | tf_op jit(solution)/shard_map/reduce_scatter | solution.py:174
  1416.4 2.0 add_convert_fusion
  (117 shorter events, 27.5 us)
Async XLA Ops:
  7.4 0.7 copy-start
  8.1 1208.9 %copy-start.3 = (bf16[256,512]{1,0:T(8,128)(2,1)S(1)}, bf16[256,512]{1,0:T(8,128)(2,1)}, u32[]{:S(2)}) copy-start(bf16[256,512]{1,0:T(8,128)(2,1)} %param.21) | copy-start | bytes 786436
  9.4 1209.0 %copy-start.1 = (bf16[512,2048]{1,0:T(8,128)(2,1)S(1)}, bf16[512,2048]{1,0:T(8,128)(2,1)}, u32[]{:S(2)}) copy-start(bf16[512,2048]{1,0:T(8,128)(2,1)} %param.14) | copy-start | bytes 6291460
  10.6 1207.8 %copy-start.6 = (bf16[2048]{0:T(1024)(128)(2,1)S(1)}, bf16[2048]{0:T(1024)(128)(2,1)}, u32[]{:S(2)}) copy-start(bf16[2048]{0:T(1024)(128)(2,1)} %param.19) | copy-start | bytes 12292
  10.6 76.7 %all-reduce.2.cloned.1.call-start = ((), (), s32[]{:S(2)}) async-start(), calls=%async_computation.5 | async-start | bytes 327680 | tf_op jit(solution)/shard_map/while/body/eval_jaxpr/psum | solution.py:24
  88.9 73.7 %all-reduce.2.cloned.1.call-start = ((), (), s32[]{:S(2)}) async-start(), calls=%async_computation.5 | async-start | bytes 327680 | tf_op jit(solution)/shard_map/while/body/eval_jaxpr/psum | solution.py:24
  164.2 73.7 %all-reduce.2.cloned.1.call-start = ((), (), s32[]{:S(2)}) async-start(), calls=%async_computation.5 | async-start | bytes 327680 | tf_op jit(solution)/shard_map/while/body/eval_jaxpr/psum | solution.py:24
  239.5 73.4 %all-reduce.2.cloned.1.call-start = ((), (), s32[]{:S(2)}) async-start(), calls=%async_computation.5 | async-start | bytes 327680 | tf_op jit(solution)/shard_map/while/body/eval_jaxpr/psum | solution.py:24
  314.5 73.4 %all-reduce.2.cloned.1.call-start = ((), (), s32[]{:S(2)}) async-start(), calls=%async_computation.5 | async-start | bytes 327680 | tf_op jit(solution)/shard_map/while/body/eval_jaxpr/psum | solution.py:24
  389.4 73.4 %all-reduce.2.cloned.1.call-start = ((), (), s32[]{:S(2)}) async-start(), calls=%async_computation.5 | async-start | bytes 327680 | tf_op jit(solution)/shard_map/while/body/eval_jaxpr/psum | solution.py:24
  464.4 73.7 %all-reduce.2.cloned.1.call-start = ((), (), s32[]{:S(2)}) async-start(), calls=%async_computation.5 | async-start | bytes 327680 | tf_op jit(solution)/shard_map/while/body/eval_jaxpr/psum | solution.py:24
  539.7 73.7 %all-reduce.2.cloned.1.call-start = ((), (), s32[]{:S(2)}) async-start(), calls=%async_computation.5 | async-start | bytes 327680 | tf_op jit(solution)/shard_map/while/body/eval_jaxpr/psum | solution.py:24
  615.0 73.7 %all-reduce.2.cloned.1.call-start = ((), (), s32[]{:S(2)}) async-start(), calls=%async_computation.5 | async-start | bytes 327680 | tf_op jit(solution)/shard_map/while/body/eval_jaxpr/psum | solution.py:24
  690.3 73.4 %all-reduce.2.cloned.1.call-start = ((), (), s32[]{:S(2)}) async-start(), calls=%async_computation.5 | async-start | bytes 327680 | tf_op jit(solution)/shard_map/while/body/eval_jaxpr/psum | solution.py:24
  765.2 73.7 %all-reduce.2.cloned.1.call-start = ((), (), s32[]{:S(2)}) async-start(), calls=%async_computation.5 | async-start | bytes 327680 | tf_op jit(solution)/shard_map/while/body/eval_jaxpr/psum | solution.py:24
  840.5 73.4 %all-reduce.2.cloned.1.call-start = ((), (), s32[]{:S(2)}) async-start(), calls=%async_computation.5 | async-start | bytes 327680 | tf_op jit(solution)/shard_map/while/body/eval_jaxpr/psum | solution.py:24
  915.5 73.7 %all-reduce.2.cloned.1.call-start = ((), (), s32[]{:S(2)}) async-start(), calls=%async_computation.5 | async-start | bytes 327680 | tf_op jit(solution)/shard_map/while/body/eval_jaxpr/psum | solution.py:24
  990.8 73.4 %all-reduce.2.cloned.1.call-start = ((), (), s32[]{:S(2)}) async-start(), calls=%async_computation.5 | async-start | bytes 327680 | tf_op jit(solution)/shard_map/while/body/eval_jaxpr/psum | solution.py:24
  1065.8 73.4 %all-reduce.2.cloned.1.call-start = ((), (), s32[]{:S(2)}) async-start(), calls=%async_computation.5 | async-start | bytes 327680 | tf_op jit(solution)/shard_map/while/body/eval_jaxpr/psum | solution.py:24
  1140.7 73.4 %all-reduce.2.cloned.1.call-start = ((), (), s32[]{:S(2)}) async-start(), calls=%async_computation.5 | async-start | bytes 327680 | tf_op jit(solution)/shard_map/while/body/eval_jaxpr/psum | solution.py:24
  1215.7 3.1 copy-start.5
  1215.7 3.1 copy-start.7
  1215.7 95.0 %all-gather.4.cloned.1.call-start = ((), (), s32[]{:S(2)}) async-start(), calls=%async_computation.1 | async-start | bytes 2359296 | tf_op jit(solution)/shard_map/all_gather | solution.py:121
  1216.3 115.3 %all-gather.6.cloned.1.call-start = ((), (), s32[]{:S(2)}) async-start(), calls=%async_computation.2 | async-start | bytes 2359296 | tf_op jit(solution)/shard_map/all_gather | solution.py:113
  1216.9 165.7 %all-gather.8.cloned.1.call-start = ((), (), s32[]{:S(2)}) async-start(), calls=%async_computation.3 | async-start | bytes 2359296 | tf_op jit(solution)/shard_map/all_gather | solution.py:171
  1217.0 9.1 collective-permute-start
  1218.3 198.2 %reduce-scatter.2.cloned.1.call-start = ((), (), s32[]{:S(2)}) async-start(), calls=%async_computation.4 | async-start | bytes 2621440 | tf_op jit(solution)/shard_map/reduce_scatter | solution.py:174
  1226.1 15.6 %collective-permute-start.1 = (bf16[256,512]{1,0:T(8,128)(2,1)S(1)}, bf16[256,512]{1,0:T(8,128)(2,1)S(1)}, u32[]{:S(2)}, u32[]{:S(2)}) collective-permute-start(bf16[256,512]{1,0:T(8,128)(2,1)S(1)} %collective-permute-done), channel_id=1, source_target_pairs={{0,4},{4,8},{8,12},{12,16},{16,20},{20,24},{24,28},{28,0},{1,5},{5... | collective-permute-start | bytes 786440 | tf_op jit(solution)/shard_map/ppermute | solution.py:17
  1241.7 9.1 collective-permute-start.2
  1250.8 16.7 %collective-permute-start.3 = (bf16[256,512]{1,0:T(8,128)(2,1)S(1)}, bf16[256,512]{1,0:T(8,128)(2,1)}, u32[]{:S(2)}, u32[]{:S(2)}) collective-permute-start(bf16[256,512]{1,0:T(8,128)(2,1)S(1)} %collective-permute-done.2), channel_id=1, source_target_pairs={{0,4},{4,8},{8,12},{12,16},{16,20},{20,24},{24,28},{28,0},{1,5},{5... | collective-permute-start | bytes 786440 | tf_op jit(solution)/shard_map/ppermute | solution.py:17
  1267.5 15.2 %collective-permute-start.4 = (bf16[256,512]{1,0:T(8,128)(2,1)}, bf16[256,512]{1,0:T(8,128)(2,1)}, u32[]{:S(2)}, u32[]{:S(2)}) collective-permute-start(bf16[256,512]{1,0:T(8,128)(2,1)} %collective-permute-done.3), channel_id=1, source_target_pairs={{0,4},{4,8},{8,12},{12,16},{16,20},{20,24},{24,28},{28,0},{1,5},{5... | collective-permute-start | bytes 786440 | tf_op jit(solution)/shard_map/ppermute | solution.py:17
  1282.7 11.2 collective-permute-start.5
  1293.9 12.1 collective-permute-start.6
  1334.6 1.4 copy-start.2
  1334.7 1.4 copy-start.4
Sparse Core Ops, SparseCore 0:
  15.1 72.1 all-reduce.1
  93.4 69.1 all-reduce.1
  168.7 69.1 all-reduce.1
  243.7 69.1 all-reduce.1
  318.7 69.1 all-reduce.1
  393.6 69.1 all-reduce.1
  469.0 69.1 all-reduce.1
  544.2 69.1 all-reduce.1
  619.5 69.1 all-reduce.1
  694.5 69.1 all-reduce.1
  769.8 69.1 all-reduce.1
  844.7 69.1 all-reduce.1
  920.0 69.1 all-reduce.1
  995.0 69.1 all-reduce.1
  1070.0 69.1 all-reduce.1
  1144.9 69.1 all-reduce.1
Sparse Core Ops, SparseCore 1:
  1218.3 58.7 all-gather.3
  1279.0 52.5 all-gather.5
  1333.5 49.0 all-gather.7
  1386.9 29.5 reduce-scatter.1
